TPU v7x, 128 devices: a whole 4x4x4 slice. The times are simulated.
128 devices in a mesh: gx: 8 (over z, x_lo), gy: 4 (over x_hi, core), ha: 4 (over y).
Axes of the slice: x: 4 (x_hi: 2, x_lo: 2; x = x_hi * 2 + x_lo), y: 4, z: 4, core: 2. Of those that a mesh axis runs over, the one named last changes fastest.
Arguments:
- tokens: bfloat16 [64, 64, 16, 384], P('gx', 'gy'), may hold values from -30 to 30
- input_weight: bfloat16 [384, 768], P(None, 'ha'), may hold values from -1 to 1
- output_weight: bfloat16 [256, 384], P('ha'), may hold values from -0.375 to 0.375
- tissue_bits: int32 [64, 64], P('gx', 'gy'), may hold values from 0 to 65535
- cotangent: bfloat16 [64, 64, 16, 384], P('gx', 'gy'), may hold values from -6 to 6
Outputs:
- token_gradient: bfloat16 [64, 64, 16, 384], P('gx', 'gy', None, 'ha')
- input_gradient: float32 [384, 768], P(None, 'ha')
- output_gradient: float32 [256, 384], P('ha')
All inputs are finite; a program needn't handle non-finite values.
Results may differ from a plain program's by a relative error of at most 0.018.
The roundings to bfloat16 on the way count: a program that leaves them out, or rounds other values in their place, can miss the bound.
Values may be sent and summed in bfloat16 or wider, within the bound.
No kernel may reach another device: no remote copies, remote signals or barrier semaphores. Data moves between devices by JAX's collectives and lax.ppermute only.
A program may use at most 128 MiB of HBM per device.

v0:
```python
import jax
import jax.numpy as jnp
from jax import lax
from jax.sharding import PartitionSpec as P

HD = 64
REACH = 3


def extended(block, sides, width):
    for axis, dim in sides:
        count = lax.axis_size(axis)
        forward = [(i, i + 1) for i in range(count - 1)]
        backward = [(target, source) for source, target in forward]
        low = lax.ppermute(
            lax.slice_in_dim(block, block.shape[dim] - width, None, axis=dim), axis, forward
        )
        high = lax.ppermute(lax.slice_in_dim(block, 0, width, axis=dim), axis, backward)
        block = jnp.concatenate([low, block, high], axis=dim)
    return block


def block_length(extent, plane_rows):
    for length in range(1, extent + 1):
        if extent % length == 0 and length * plane_rows >= 512:
            return length
    return extent


def shards(tokens, input_weight, output_weight, tissue_bits, cotangent):
    width_x, width_y, depth, model_width = tokens.shape
    local_heads = output_weight.shape[0] // HD
    token_count = width_x * width_y * depth
    score_scale = HD ** (-0.5)
    flat_tokens = tokens.reshape(token_count, model_width)
    flat_cotangent = cotangent.reshape(token_count, model_width)
    bit_values = 2 ** jnp.arange(depth, dtype=jnp.int32)
    key_valid = (tissue_bits[:, :, None] // bit_values % 2).astype(jnp.bfloat16)
    key_span_x_full = width_x + 2 * REACH
    key_span_y = width_y + 2 * REACH
    projected = jnp.dot(flat_tokens, input_weight, preferred_element_type=jnp.float32).astype(
        jnp.bfloat16
    )
    projected = projected.reshape(token_count, local_heads, 3, HD)
    queries = projected[:, :, 0, :].reshape(token_count, local_heads * HD)
    pair_local = projected[:, :, 1:, :].reshape(width_x, width_y, depth, local_heads * 2 * HD)
    pair_padded, valid_padded = (
        extended(pair_local, (("gx", 0), ("gy", 1)), REACH),
        extended(key_valid, (("gx", 0), ("gy", 1)), REACH),
    )
    upstream = jnp.einsum(
        "nd,ed->ne", flat_cotangent, output_weight, preferred_element_type=jnp.float32
    ).astype(jnp.bfloat16)
    block_x = block_length(width_x, width_y * depth)
    block_count = width_x // block_x
    key_span_x = block_x + 2 * REACH
    query_rows = block_x * width_y * depth
    key_rows = key_span_x * key_span_y * depth
    query_slots = jnp.arange(query_rows)
    query_x = query_slots // (width_y * depth)
    query_y = query_slots // depth % width_y
    query_z = query_slots % depth
    key_slots = jnp.arange(key_rows)
    key_x = key_slots // (key_span_y * depth) - REACH
    key_y = key_slots // depth % key_span_y - REACH
    key_z = key_slots % depth
    within = (
        (jnp.abs(query_x[:, None] - key_x[None, :]) <= REACH)
        & (jnp.abs(query_y[:, None] - key_y[None, :]) <= REACH)
        & (jnp.abs(query_z[:, None] - key_z[None, :]) <= REACH)
    )
    self_pair = (
        (query_x[:, None] == key_x[None, :])
        & (query_y[:, None] == key_y[None, :])
        & (query_z[:, None] == key_z[None, :])
    )
    query_grid = queries.reshape(width_x, width_y, depth, local_heads, HD)
    upstream_grid = upstream.reshape(width_x, width_y, depth, local_heads, HD)
    pair_grid = pair_padded.reshape(key_span_x_full, key_span_y, depth, local_heads, 2, HD)

    def attend_block(block_index, carry):
        query_sums, pair_sums, outputs = carry
        first_row = block_index * block_x
        query_block = lax.dynamic_slice_in_dim(query_grid, first_row, block_x, 0).reshape(
            query_rows, local_heads, HD
        )
        upstream_block = lax.dynamic_slice_in_dim(upstream_grid, first_row, block_x, 0).reshape(
            query_rows, local_heads, HD
        )
        pair_block = lax.dynamic_slice_in_dim(pair_grid, first_row, key_span_x, 0).reshape(
            key_rows, local_heads, 2, HD
        )
        keys_block = pair_block[:, :, 0, :]
        values_block = pair_block[:, :, 1, :]
        live_keys = (
            lax.dynamic_slice_in_dim(valid_padded, first_row, key_span_x, 0).reshape(key_rows) > 0
        )
        allowed = within & (live_keys[None, :] | self_pair)
        scores = (
            jnp.einsum("qhe,khe->hqk", query_block, keys_block, preferred_element_type=jnp.float32)
            * score_scale
        )
        scores = jnp.where(allowed[None], scores, -jnp.inf)
        row_max = jnp.max(scores, axis=-1, keepdims=True)
        raised = jnp.exp(scores - row_max)
        weights = (raised / jnp.sum(raised, axis=-1, keepdims=True)).astype(jnp.bfloat16)
        result = jnp.einsum(
            "hqk,khe->qhe", weights, values_block, preferred_element_type=jnp.float32
        )
        weight_gradient = jnp.einsum(
            "qhe,khe->hqk", upstream_block, values_block, preferred_element_type=jnp.float32
        )
        row_inner = jnp.sum(upstream_block.astype(jnp.float32) * result, axis=-1)
        score_gradient = (
            weights.astype(jnp.float32) * (weight_gradient - row_inner.T[:, :, None]) * score_scale
        ).astype(jnp.bfloat16)
        query_gradient = jnp.einsum(
            "hqk,khe->qhe", score_gradient, keys_block, preferred_element_type=jnp.float32
        )
        key_gradient = jnp.einsum(
            "hqk,qhe->khe", score_gradient, query_block, preferred_element_type=jnp.float32
        )
        value_gradient = jnp.einsum(
            "hqk,qhe->khe", weights, upstream_block, preferred_element_type=jnp.float32
        )
        pair_gradient = jnp.stack([key_gradient, value_gradient], axis=2).reshape(
            key_span_x, key_span_y, depth, local_heads * 2 * HD
        )
        query_sums = lax.dynamic_update_slice_in_dim(
            query_sums,
            query_gradient.reshape(block_x, width_y, depth, local_heads * HD),
            first_row,
            0,
        )
        previous = lax.dynamic_slice_in_dim(pair_sums, first_row, key_span_x, 0)
        pair_sums = lax.dynamic_update_slice_in_dim(
            pair_sums, previous + pair_gradient, first_row, 0
        )
        outputs = lax.dynamic_update_slice_in_dim(
            outputs,
            result.astype(jnp.bfloat16).reshape(block_x, width_y, depth, local_heads * HD),
            first_row,
            0,
        )
        return (query_sums, pair_sums, outputs)

    start = (
        jnp.zeros((width_x, width_y, depth, local_heads * HD), jnp.float32),
        jnp.zeros((key_span_x_full, key_span_y, depth, local_heads * 2 * HD), jnp.float32),
        jnp.zeros((width_x, width_y, depth, local_heads * HD), jnp.bfloat16),
    )
    query_sums, pair_sums, outputs = lax.fori_loop(0, block_count, attend_block, start)
    rims_first = jnp.concatenate([pair_sums[:REACH], pair_sums[width_x + REACH :]], axis=0)
    from_first = extended(rims_first.astype(jnp.bfloat16), (("gx", 0),), REACH).astype(
        rims_first.dtype
    )
    interior = pair_sums[REACH : width_x + REACH]
    interior = interior.at[:REACH].add(from_first[:REACH])
    interior = interior.at[width_x - REACH :].add(from_first[3 * REACH :])
    rims_second = jnp.concatenate([interior[:, :REACH], interior[:, width_y + REACH :]], axis=1)
    from_second = extended(rims_second.astype(jnp.bfloat16), (("gy", 1),), REACH).astype(
        rims_second.dtype
    )
    centre = interior[:, REACH : width_y + REACH]
    centre = centre.at[:, :REACH].add(from_second[:, :REACH])
    centre = centre.at[:, width_y - REACH :].add(from_second[:, 3 * REACH :])
    query_part = query_sums.reshape(token_count, local_heads, 1, HD)
    pair_part = centre.reshape(token_count, local_heads, 2, HD)
    dprojected = (
        jnp.concatenate([query_part, pair_part], axis=2)
        .reshape(token_count, local_heads * 3 * HD)
        .astype(jnp.bfloat16)
    )
    partial_terms = jnp.einsum(
        "nc,dc->nd", dprojected, input_weight, preferred_element_type=jnp.float32
    ).reshape(width_x, width_y, depth, model_width)
    token_gradient = lax.psum_scatter(partial_terms, "ha", scatter_dimension=3, tiled=True).astype(
        jnp.bfloat16
    )
    attended_flat = outputs.reshape(token_count, local_heads * HD)
    part_input = jnp.einsum(
        "nd,nc->dc", flat_tokens, dprojected, preferred_element_type=jnp.float32
    )
    part_output = jnp.einsum(
        "ne,nd->ed", attended_flat, flat_cotangent, preferred_element_type=jnp.float32
    )
    summed_input, summed_output = (
        lax.psum(part_input.astype(jnp.bfloat16), ("gx", "gy")).astype(jnp.float32),
        lax.psum(part_output.astype(jnp.bfloat16), ("gx", "gy")).astype(jnp.float32),
    )
    normaliser = (token_count * lax.axis_size("gx") * lax.axis_size("gy")) ** (-0.5)
    return (token_gradient, summed_input * normaliser, summed_output * normaliser)


def solution(mesh):
    placed = (
        P("gx", "gy", None, None),
        P(None, "ha"),
        P("ha", None),
        P("gx", "gy"),
        P("gx", "gy", None, None),
    )
    return jax.shard_map(
        shards,
        mesh=mesh,
        in_specs=placed,
        out_specs=(P("gx", "gy", None, "ha"), P(None, "ha"), P("ha", None)),
        check_vma=False,
    )
```

profile of v0, /device:TPU:0, one launch (start us, length us, event | category | flops | bytes accessed | tf_op | source)
XLA Modules:
  0.0 429.6 jit_solution(15858001204018962524)
XLA Ops:
  11.0 3.5 collective-permute-start.4
  24.8 5.9 %collective-permute-start = (bf16[3,16,16,128]{3,2,1,0:T(8,128)(2,1)}, bf16[3,16,16,128]{3,2,1,0:T(8,128)(2,1)}, u32[]{:S(2)}, u32[]{:S(2)}) collective-permute-start(bf16[3,16,16,128]{3,2,1,0:T(8,128)(2,1)} %slice.209), channel_id=1, source_target_pairs={{0,16},{16,32},{32,48},{48,64},{64,80},{80,96},{96,112},{1,17},{17... | collective-permute-start | bytes 589832 | tf_op jit(solution)/shard_map/ppermute | solution.py:15
  41.4 6.2 %collective-permute-start.2 = (bf16[14,3,16,128]{3,2,1,0:T(8,128)(2,1)S(1)}, bf16[14,3,16,128]{3,2,1,0:T(8,128)(2,1)S(1)}, u32[]{:S(2)}, u32[]{:S(2)}) collective-permute-start(bf16[14,3,16,128]{3,2,1,0:T(8,128)(2,1)S(1)} %get-tuple-element.401), channel_id=1, source_target_pairs={{0,4},{4,8},{8,12},{1,5},{5,9},{9,13},{2,6},{6,10},{10,14},{3,7},{... | collective-permute-start | bytes 516104 | tf_op jit(solution)/shard_map/ppermute | solution.py:15
  60.7 128.2 %while.23 = (s32[]{:T(128)}, bf16[8,16,16,64]{3,2,1,0:T(8,128)(2,1)}, f32[14,22,16,128]{3,2,1,0:T(8,128)}, bf16[8,16,16,64]{3,2,1,0:T(8,128)(2,1)}, bf16[14,22,1...) while((s32[]{:T(128)}, ...), condition=%wide.region_4.5_spmd.clone.clone, body=%wide.region_0.4_spmd.clone.clone.sunk | while | flops 1152845056 | bytes 82846784 | solution.py:152
  66.3 5.8 %fusion.85 = (f32[512]{0:T(512)S(1)}, f32[512,2816]{1,0:T(8,128)S(1)}) fusion(bf16[512,64]{1,0:T(8,128)(2,1)S(1)} %bitcast.150, bf16[2816,1,2,64]{3,0,2,1:T(8,128)(2,1)S(1)} %bitcast.143, pred[2816]{0:T(1024)(128)(4,1)S(1)} %gt.22, s32[2816]{0:T(1024)S(1)} %get-tuple-element.564, s32[512]{0:T(512)S(1)} %get-tuple-element.565, ...), kind=kOutput, calls=%fused_computation.123.clone.1 | convolution fusion | flops 214826496 | bytes 6667264 | tf_op jit(solution)/shard_map/while/body/eval_jaxpr/qhe,khe->hqk/dot_general | solution.py:100
  77.2 2.6 convolution_bitcast_fusion.9
  83.6 3.3 copy.74
  86.9 3.2 reshape.514
  90.1 2.7 add_dynamic-update-slice_fusion.2
  98.4 5.8 %fusion.85 = (f32[512]{0:T(512)S(1)}, f32[512,2816]{1,0:T(8,128)S(1)}) fusion(bf16[512,64]{1,0:T(8,128)(2,1)S(1)} %bitcast.150, bf16[2816,1,2,64]{3,0,2,1:T(8,128)(2,1)S(1)} %bitcast.143, pred[2816]{0:T(1024)(128)(4,1)S(1)} %gt.22, s32[2816]{0:T(1024)S(1)} %get-tuple-element.564, s32[512]{0:T(512)S(1)} %get-tuple-element.565, ...), kind=kOutput, calls=%fused_computation.123.clone.1 | convolution fusion | flops 214826496 | bytes 6667264 | tf_op jit(solution)/shard_map/while/body/eval_jaxpr/qhe,khe->hqk/dot_general | solution.py:100
  115.7 3.3 copy.74
  119.0 3.2 reshape.514
  122.2 2.7 add_dynamic-update-slice_fusion.2
  130.4 5.8 %fusion.85 = (f32[512]{0:T(512)S(1)}, f32[512,2816]{1,0:T(8,128)S(1)}) fusion(bf16[512,64]{1,0:T(8,128)(2,1)S(1)} %bitcast.150, bf16[2816,1,2,64]{3,0,2,1:T(8,128)(2,1)S(1)} %bitcast.143, pred[2816]{0:T(1024)(128)(4,1)S(1)} %gt.22, s32[2816]{0:T(1024)S(1)} %get-tuple-element.564, s32[512]{0:T(512)S(1)} %get-tuple-element.565, ...), kind=kOutput, calls=%fused_computation.123.clone.1 | convolution fusion | flops 214826496 | bytes 6667264 | tf_op jit(solution)/shard_map/while/body/eval_jaxpr/qhe,khe->hqk/dot_general | solution.py:100
  141.4 2.6 convolution_bitcast_fusion.9
  147.8 3.3 copy.74
  151.0 3.2 reshape.514
  154.2 2.7 add_dynamic-update-slice_fusion.2
  162.5 5.8 %fusion.85 = (f32[512]{0:T(512)S(1)}, f32[512,2816]{1,0:T(8,128)S(1)}) fusion(bf16[512,64]{1,0:T(8,128)(2,1)S(1)} %bitcast.150, bf16[2816,1,2,64]{3,0,2,1:T(8,128)(2,1)S(1)} %bitcast.143, pred[2816]{0:T(1024)(128)(4,1)S(1)} %gt.22, s32[2816]{0:T(1024)S(1)} %get-tuple-element.564, s32[512]{0:T(512)S(1)} %get-tuple-element.565, ...), kind=kOutput, calls=%fused_computation.123.clone.1 | convolution fusion | flops 214826496 | bytes 6667264 | tf_op jit(solution)/shard_map/while/body/eval_jaxpr/qhe,khe->hqk/dot_general | solution.py:100
  179.8 3.3 copy.74
  183.1 3.2 reshape.514
  186.3 2.7 add_dynamic-update-slice_fusion.2
  191.0 3.6 collective-permute-start.8
  198.5 7.3 %collective-permute-done.9 = bf16[3,22,16,128]{3,2,1,0:T(8,128)(2,1)S(1)} collective-permute-done((bf16[3,22,16,128]{3,2,1,0:T(8,128)(2,1)S(1)}, bf16[3,22,16,128]{3,2,1,0:T(8,128)(2,1)S(1)}, u32[]{:S(2)}, u32[]{:S(2)}) %collective-permute-start.9) | collective-permute-done | bytes 270368 | tf_op jit(solution)/shard_map/ppermute | solution.py:18
  206.8 6.8 %collective-permute-start.10 = (bf16[8,3,16,128]{3,2,1,0:T(8,128)(2,1)}, bf16[8,3,16,128]{3,2,1,0:T(8,128)(2,1)}, u32[]{:S(2)}, u32[]{:S(2)}) collective-permute-start(bf16[8,3,16,128]{3,2,1,0:T(8,128)(2,1)} %get-tuple-element.405), channel_id=1, source_target_pairs={{0,4},{4,8},{8,12},{1,5},{5,9},{9,13},{2,6},{6,10},{10,14},{3,7},{... | collective-permute-start | bytes 294920 | tf_op jit(solution)/shard_map/ppermute | solution.py:15
  216.9 3.0 collective-permute-done.11
  230.4 4.1 convert_element_type.112
  236.9 20.4 %copy.58 = f32[8,16,16,384]{2,1,0,3:T(8,128)} copy(f32[8,16,16,384]{3,2,1,0:T(8,128)} %fusion.14) | data formatting | bytes 6291456
  257.2 21.8 %reshape.511 = f32[384,2048]{1,0:T(8,128)} reshape(f32[384,8,16,16]{3,2,1,0:T(8,128)} %bitcast.147) | data formatting | bytes 6291456
  281.9 128.5 %psum.15 = bf16[64,384]{1,0:T(8,128)(2,1)S(1)} all-reduce(bf16[64,384]{1,0:T(8,128)(2,1)S(1)} %fusion.9), channel_id=1, replica_groups=mesh['gx'=8,'gy'=4,'ha'=4] {'gx','gy'}, use_global_device_ids=true, to_apply=%region_7.8 | all-reduce | flops 24576 | bytes 98304 | tf_op jit(solution)/shard_map/psum | solution.py:189
  412.7 4.7 %reshape.512 = bf16[96,8,16,16]{3,2,1,0:T(8,128)(2,1)} reshape(f32[96,2048]{1,0:T(8,128)} %reduce-scatter.4.cloned.1.call-done) | data formatting | bytes 1179648
  417.4 4.8 %copy.59 = bf16[8,16,16,96]{3,2,1,0:T(8,128)(2,1)} copy(bf16[8,16,16,96]{2,1,0,3:T(8,128)(2,1)} %bitcast.154) | data formatting | bytes 786432
  (189 shorter events, 127.9 us)
Async XLA Ops:
  8.0 7.8 %copy-start = (bf16[8,16,16,384]{3,2,1,0:T(8,128)(2,1)S(1)}, bf16[8,16,16,384]{3,2,1,0:T(8,128)(2,1)}, u32[]{:S(2)}) copy-start(bf16[8,16,16,384]{3,2,1,0:T(8,128)(2,1)} %param.15) | copy-start | bytes 4718596
  8.0 403.1 %all-reduce.2.cloned.1.call-start = ((), (), s32[]{:S(2)}) async-start(), calls=%async_computation.1 | async-start | bytes 294912 | tf_op jit(solution)/shard_map/psum | solution.py:188
  10.3 5.4 %copy-start.11 = (bf16[8,16,16]{2,1,0:T(8,128)(2,1)}, bf16[8,16,16]{2,1,0:T(8,128)(2,1)S(1)}, u32[]{:S(2)}) copy-start(bf16[8,16,16]{2,1,0:T(8,128)(2,1)S(1)} %fusion.17) | copy-start | bytes 12292
  11.0 24.1 %collective-permute-start.4 = (bf16[3,16,16]{2,1,0:T(8,128)(2,1)}, bf16[3,16,16]{2,1,0:T(8,128)(2,1)S(1)}, u32[]{:S(2)}, u32[]{:S(2)}) collective-permute-start(bf16[3,16,16]{2,1,0:T(8,128)(2,1)} %get-tuple-element.409), channel_id=1, source_target_pairs={{0,16},{16,32},{32,48},{48,64},{64,80},{80,96},{96,112},{1,17},{17... | collective-permute-start | bytes 4616 | tf_op jit(solution)/shard_map/ppermute | solution.py:15
  14.5 20.6 %collective-permute-start.5 = (bf16[3,16,16]{2,1,0:T(8,128)(2,1)}, bf16[3,16,16]{2,1,0:T(8,128)(2,1)}, u32[]{:S(2)}, u32[]{:S(2)}) collective-permute-start(bf16[3,16,16]{2,1,0:T(8,128)(2,1)} %get-tuple-element.410), channel_id=1, source_target_pairs={{16,0},{32,16},{48,32},{64,48},{80,64},{96,80},{112,96},{17,1},{33... | collective-permute-start | bytes 4616 | tf_op jit(solution)/shard_map/ppermute | solution.py:18
  15.8 15.5 %copy-start.4 = (bf16[8,16,16,384]{3,2,1,0:T(8,128)(2,1)S(1)}, bf16[8,16,16,384]{3,2,1,0:T(8,128)(2,1)}, u32[]{:S(2)}) copy-start(bf16[8,16,16,384]{3,2,1,0:T(8,128)(2,1)} %param.19) | copy-start | bytes 4718596
  21.4 18.1 %collective-permute-start.1 = (bf16[3,16,16,128]{3,2,1,0:T(8,128)(2,1)}, bf16[3,16,16,128]{3,2,1,0:T(8,128)(2,1)}, u32[]{:S(2)}, u32[]{:S(2)}) collective-permute-start(bf16[3,16,16,128]{3,2,1,0:T(8,128)(2,1)} %slice.212), channel_id=1, source_target_pairs={{16,0},{32,16},{48,32},{64,48},{80,64},{96,80},{112,96},{17,1},{33... | collective-permute-start | bytes 589832 | tf_op jit(solution)/shard_map/ppermute | solution.py:18
  24.8 13.6 %collective-permute-start = (bf16[3,16,16,128]{3,2,1,0:T(8,128)(2,1)}, bf16[3,16,16,128]{3,2,1,0:T(8,128)(2,1)}, u32[]{:S(2)}, u32[]{:S(2)}) collective-permute-start(bf16[3,16,16,128]{3,2,1,0:T(8,128)(2,1)} %slice.209), channel_id=1, source_target_pairs={{0,16},{16,32},{32,48},{48,64},{64,80},{80,96},{96,112},{1,17},{17... | collective-permute-start | bytes 589832 | tf_op jit(solution)/shard_map/ppermute | solution.py:15
  32.7 2.4 copy-start.12
  35.8 16.2 %collective-permute-start.6 = (bf16[14,3,16]{2,1,0:T(4,128)(2,1)S(1)}, bf16[14,3,16]{2,1,0:T(4,128)(2,1)S(1)}, u32[]{:S(2)}, u32[]{:S(2)}) collective-permute-start(bf16[14,3,16]{2,1,0:T(4,128)(2,1)S(1)} %get-tuple-element.407), channel_id=1, source_target_pairs={{0,4},{4,8},{8,12},{1,5},{5,9},{9,13},{2,6},{6,10},{10,14},{3,7},{... | collective-permute-start | bytes 4040 | tf_op jit(solution)/shard_map/ppermute | solution.py:15
  37.1 14.9 %collective-permute-start.7 = (bf16[14,3,16]{2,1,0:T(4,128)(2,1)S(1)}, bf16[14,3,16]{2,1,0:T(4,128)(2,1)S(1)}, u32[]{:S(2)}, u32[]{:S(2)}) collective-permute-start(bf16[14,3,16]{2,1,0:T(4,128)(2,1)S(1)} %get-tuple-element.408), channel_id=1, source_target_pairs={{4,0},{8,4},{12,8},{5,1},{9,5},{13,9},{6,2},{10,6},{14,10},{7,3},{... | collective-permute-start | bytes 4040 | tf_op jit(solution)/shard_map/ppermute | solution.py:18
  41.4 12.0 %collective-permute-start.2 = (bf16[14,3,16,128]{3,2,1,0:T(8,128)(2,1)S(1)}, bf16[14,3,16,128]{3,2,1,0:T(8,128)(2,1)S(1)}, u32[]{:S(2)}, u32[]{:S(2)}) collective-permute-start(bf16[14,3,16,128]{3,2,1,0:T(8,128)(2,1)S(1)} %get-tuple-element.401), channel_id=1, source_target_pairs={{0,4},{4,8},{8,12},{1,5},{5,9},{9,13},{2,6},{6,10},{10,14},{3,7},{... | collective-permute-start | bytes 516104 | tf_op jit(solution)/shard_map/ppermute | solution.py:15
  47.5 6.2 %collective-permute-start.3 = (bf16[14,3,16,128]{3,2,1,0:T(8,128)(2,1)S(1)}, bf16[14,3,16,128]{3,2,1,0:T(8,128)(2,1)}, u32[]{:S(2)}, u32[]{:S(2)}) collective-permute-start(bf16[14,3,16,128]{3,2,1,0:T(8,128)(2,1)S(1)} %get-tuple-element.402), channel_id=1, source_target_pairs={{4,0},{8,4},{12,8},{5,1},{9,5},{13,9},{6,2},{10,6},{14,10},{7,3},{... | collective-permute-start | bytes 516104 | tf_op jit(solution)/shard_map/ppermute | solution.py:18
  57.2 3.5 copy-start.13
  74.5 1.5 copy-start.1
  77.2 2.7 copy-start.2
  106.6 1.5 copy-start.1
  109.3 2.7 copy-start.2
  138.7 1.5 copy-start.1
  141.4 2.7 copy-start.2
  170.7 1.5 copy-start.1
  173.4 2.7 copy-start.2
  188.9 7.0 %copy-start.3 = (f32[14,22,16,128]{3,2,1,0:T(8,128)S(1)}, f32[14,22,16,128]{3,2,1,0:T(8,128)}, u32[]{:S(2)}) copy-start(f32[14,22,16,128]{3,2,1,0:T(8,128)} %get-tuple-element.223) | copy-start | bytes 7569412
  191.0 7.5 %collective-permute-start.8 = (bf16[3,22,16,128]{3,2,1,0:T(8,128)(2,1)S(1)}, bf16[3,22,16,128]{3,2,1,0:T(8,128)(2,1)S(1)}, u32[]{:S(2)}, u32[]{:S(2)}) collective-permute-start(bf16[3,22,16,128]{3,2,1,0:T(8,128)(2,1)S(1)} %get-tuple-element.399), channel_id=1, source_target_pairs={{0,16},{16,32},{32,48},{48,64},{64,80},{80,96},{96,112},{1,17},{17... | collective-permute-start | bytes 811016 | tf_op jit(solution)/shard_map/ppermute | solution.py:15
  194.6 11.3 %collective-permute-start.9 = (bf16[3,22,16,128]{3,2,1,0:T(8,128)(2,1)S(1)}, bf16[3,22,16,128]{3,2,1,0:T(8,128)(2,1)S(1)}, u32[]{:S(2)}, u32[]{:S(2)}) collective-permute-start(bf16[3,22,16,128]{3,2,1,0:T(8,128)(2,1)S(1)} %get-tuple-element.400), channel_id=1, source_target_pairs={{16,0},{32,16},{48,32},{64,48},{80,64},{96,80},{112,96},{17,1},{33... | collective-permute-start | bytes 811016 | tf_op jit(solution)/shard_map/ppermute | solution.py:18
  205.9 9.0 %copy-start.8 = (bf16[8,16,16,64]{3,2,1,0:T(8,128)(2,1)S(1)}, bf16[8,16,16,64]{3,2,1,0:T(8,128)(2,1)}, u32[]{:S(2)}) copy-start(bf16[8,16,16,64]{3,2,1,0:T(8,128)(2,1)} %get-tuple-element.222) | copy-start | bytes 786436
  206.8 10.1 %collective-permute-start.10 = (bf16[8,3,16,128]{3,2,1,0:T(8,128)(2,1)}, bf16[8,3,16,128]{3,2,1,0:T(8,128)(2,1)}, u32[]{:S(2)}, u32[]{:S(2)}) collective-permute-start(bf16[8,3,16,128]{3,2,1,0:T(8,128)(2,1)} %get-tuple-element.405), channel_id=1, source_target_pairs={{0,4},{4,8},{8,12},{1,5},{5,9},{9,13},{2,6},{6,10},{10,14},{3,7},{... | collective-permute-start | bytes 294920 | tf_op jit(solution)/shard_map/ppermute | solution.py:15
  213.6 6.3 %collective-permute-start.11 = (bf16[8,3,16,128]{3,2,1,0:T(8,128)(2,1)}, bf16[8,3,16,128]{3,2,1,0:T(8,128)(2,1)}, u32[]{:S(2)}, u32[]{:S(2)}) collective-permute-start(bf16[8,3,16,128]{3,2,1,0:T(8,128)(2,1)} %get-tuple-element.406), channel_id=1, source_target_pairs={{4,0},{8,4},{12,8},{5,1},{9,5},{13,9},{6,2},{10,6},{14,10},{7,3},{... | collective-permute-start | bytes 294920 | tf_op jit(solution)/shard_map/ppermute | solution.py:18
  216.9 9.6 %copy-start.9 = (bf16[2048,1,1,64]{0,3,2,1:T(8,128)(2,1)S(1)}, bf16[2048,1,1,64]{0,3,2,1:T(8,128)(2,1)}, u32[]{:S(2)}) copy-start(bf16[2048,1,1,64]{0,3,2,1:T(8,128)(2,1)} %copy.53) | copy-start | bytes 786436
  229.1 5.4 %copy-start.10 = (bf16[384,192]{0,1:T(8,128)(2,1)S(1)}, bf16[384,192]{0,1:T(8,128)(2,1)}, u32[]{:S(2)}) copy-start(bf16[384,192]{0,1:T(8,128)(2,1)} %param.16) | copy-start | bytes 442372
  230.3 182.4 %reduce-scatter.4.cloned.1.call-start = ((), (), s32[]{:S(2)}) async-start(), calls=%async_computation.2 | async-start | bytes 3932160
  279.1 1.4 copy-start.5
  (2 other events, 1.9 us)
Sparse Core Ops, SparseCore 0:
  230.5 102.9 all-reduce.1
Sparse Core Ops, SparseCore 1:
  279.2 42.6 reduce-scatter.3
where the time goes:
time: 432 us; the launch traced here: 430 us
  local copies, waits for them, and re-layouts  141 us (33%)
  blocking collectives  129 us (30%)
  matrix products  57 us (13%)
  other arithmetic  38.5 us (9%)
  starting transfers between devices  35 us (8%)
  between operations  15.9 us (4%)
  waiting for transfers between devices  13.2 us (3%)
    psum x1, blocking collectives, shards(): lax.psum(part_output.astype(jnp.bfloat16), ('gx', 'gy')).astype(jnp.float32)  129 us
    unnamed x34, local copies, waits for them, and re-layouts  60.2 us
    ppermute x6, starting transfers between devices, extended(): lax.ppermute(lax.slice_in_dim(block, block.shape[dim] - width, None, axis...  27.2 us
    dot_general x4, matrix products, attend_block(): jnp.einsum('qhe,khe->hqk', query_block, keys_block, preferred_element_typ...  23.3 us
    another operation x4, local copies, waits for them, and re-layouts, attend_block(): jnp.stack([key_gradient, value_gradient], axis=2)  13.1 us
    reshape x4, local copies, waits for them, and re-layouts, attend_block(): jnp.stack([key_gradient, value_gradient], axis=2)  12.6 us
    dynamic_update_slice x4, other arithmetic, attend_block(): lax.dynamic_update_slice_in_dim(pair_sums, previous + pair_gradient, firs...  10.7 us
    ppermute x6, waiting for transfers between devices, extended(): lax.ppermute(lax.slice_in_dim(block, 0, width, axis=dim), axis, backward)  10.7 us
  transfers between devices with their start and end apart: 14, of which 4 were waited for; matrix products, arithmetic and copies ran while one was open for 17% of the time, Pallas kernels for 0%

commit v1 on v0

--- a/solution.py
+++ b/solution.py
@@ -186,7 +186,9 @@
     )
     summed_input, summed_output = (
         lax.psum(part_input.astype(jnp.bfloat16), ("gx", "gy")).astype(jnp.float32),
-        lax.psum(part_output.astype(jnp.bfloat16), ("gx", "gy")).astype(jnp.float32),
+        lax.psum(lax.psum(part_output.astype(jnp.bfloat16), axis_name="gx"), axis_name="gy").astype(
+            jnp.float32
+        ),
     )
     normaliser = (token_count * lax.axis_size("gx") * lax.axis_size("gy")) ** (-0.5)
     return (token_gradient, summed_input * normaliser, summed_output * normaliser)

time: 432 us -> 357 us (0.83)
  blocking collectives: 129 us -> 47.4 us
    psum x1 -> x2, blocking collectives: 129 us -> 47.4 us  [the longest x1 32.6 us: shards(): lax.psum(part_output.astype(jnp.bfloat16), axis_name='gx')]
  transfers between devices with their start and end apart: 14 -> 14, of which waited for: 4 -> 5; matrix products, arithmetic and copies ran while one was open for 17% -> 21% of each run, Pallas kernels for 0% -> 0%
where the time goes in v1:
time: 357 us; the launch traced here: 352 us
  local copies, waits for them, and re-layouts  141 us (39%)
  matrix products  57 us (16%)
  blocking collectives  47.4 us (13%)
  other arithmetic  38.4 us (11%)
  starting transfers between devices  35 us (10%)
  waiting for transfers between devices  16.7 us (5%)
  between operations  15.9 us (4%)
    unnamed x34, local copies, waits for them, and re-layouts  60.3 us
    psum x1, blocking collectives, shards(): lax.psum(part_output.astype(jnp.bfloat16), axis_name='gx')  32.6 us
    ppermute x6, starting transfers between devices, extended(): lax.ppermute(lax.slice_in_dim(block, block.shape[dim] - width, None, axis...  27.2 us
    dot_general x4, matrix products, attend_block(): jnp.einsum('qhe,khe->hqk', query_block, keys_block, preferred_element_typ...  23.3 us
    psum x1, blocking collectives, shards(): lax.psum(lax.psum(part_output.astype(jnp.bfloat16), axis_name='gx'), axis...  14.8 us
    another operation x4, local copies, waits for them, and re-layouts, attend_block(): jnp.stack([key_gradient, value_gradient], axis=2)  13.2 us
    reshape x4, local copies, waits for them, and re-layouts, attend_block(): jnp.stack([key_gradient, value_gradient], axis=2)  12.6 us
    ppermute x6, waiting for transfers between devices, extended(): lax.ppermute(lax.slice_in_dim(block, 0, width, axis=dim), axis, backward)  10.7 us
  transfers between devices with their start and end apart: 14, of which 5 were waited for; matrix products, arithmetic and copies ran while one was open for 21% of the time, Pallas kernels for 0%

profile of v1, /device:TPU:0, one launch (start us, length us, event | category | flops | bytes accessed | tf_op | source)
XLA Modules:
  0.0 352.1 jit_solution(9443819936808401283)
XLA Ops:
  11.0 3.5 collective-permute-start.4
  24.8 5.8 %collective-permute-start = (bf16[3,16,16,128]{3,2,1,0:T(8,128)(2,1)}, bf16[3,16,16,128]{3,2,1,0:T(8,128)(2,1)}, u32[]{:S(2)}, u32[]{:S(2)}) collective-permute-start(bf16[3,16,16,128]{3,2,1,0:T(8,128)(2,1)} %slice.209), channel_id=1, source_target_pairs={{0,16},{16,32},{32,48},{48,64},{64,80},{80,96},{96,112},{1,17},{17... | collective-permute-start | bytes 589832 | tf_op jit(solution)/shard_map/ppermute | solution.py:15
  41.4 6.2 %collective-permute-start.2 = (bf16[14,3,16,128]{3,2,1,0:T(8,128)(2,1)S(1)}, bf16[14,3,16,128]{3,2,1,0:T(8,128)(2,1)S(1)}, u32[]{:S(2)}, u32[]{:S(2)}) collective-permute-start(bf16[14,3,16,128]{3,2,1,0:T(8,128)(2,1)S(1)} %get-tuple-element.401), channel_id=1, source_target_pairs={{0,4},{4,8},{8,12},{1,5},{5,9},{9,13},{2,6},{6,10},{10,14},{3,7},{... | collective-permute-start | bytes 516104 | tf_op jit(solution)/shard_map/ppermute | solution.py:15
  60.7 128.3 %while.23 = (s32[]{:T(128)}, bf16[8,16,16,64]{3,2,1,0:T(8,128)(2,1)}, f32[14,22,16,128]{3,2,1,0:T(8,128)}, bf16[8,16,16,64]{3,2,1,0:T(8,128)(2,1)}, bf16[14,22,1...) while((s32[]{:T(128)}, ...), condition=%wide.region_4.5_spmd.clone.clone, body=%wide.region_0.4_spmd.clone.clone.sunk | while | flops 1152845056 | bytes 82846784 | solution.py:152
  66.3 5.8 %fusion.85 = (f32[512]{0:T(512)S(1)}, f32[512,2816]{1,0:T(8,128)S(1)}) fusion(bf16[512,64]{1,0:T(8,128)(2,1)S(1)} %bitcast.150, bf16[2816,1,2,64]{3,0,2,1:T(8,128)(2,1)S(1)} %bitcast.143, pred[2816]{0:T(1024)(128)(4,1)S(1)} %gt.22, s32[2816]{0:T(1024)S(1)} %get-tuple-element.564, s32[512]{0:T(512)S(1)} %get-tuple-element.565, ...), kind=kOutput, calls=%fused_computation.123.clone.1 | convolution fusion | flops 214826496 | bytes 6667264 | tf_op jit(solution)/shard_map/while/body/eval_jaxpr/qhe,khe->hqk/dot_general | solution.py:100
  83.7 3.3 copy.74
  87.0 3.2 reshape.514
  90.1 2.7 add_dynamic-update-slice_fusion.2
  98.4 5.8 %fusion.85 = (f32[512]{0:T(512)S(1)}, f32[512,2816]{1,0:T(8,128)S(1)}) fusion(bf16[512,64]{1,0:T(8,128)(2,1)S(1)} %bitcast.150, bf16[2816,1,2,64]{3,0,2,1:T(8,128)(2,1)S(1)} %bitcast.143, pred[2816]{0:T(1024)(128)(4,1)S(1)} %gt.22, s32[2816]{0:T(1024)S(1)} %get-tuple-element.564, s32[512]{0:T(512)S(1)} %get-tuple-element.565, ...), kind=kOutput, calls=%fused_computation.123.clone.1 | convolution fusion | flops 214826496 | bytes 6667264 | tf_op jit(solution)/shard_map/while/body/eval_jaxpr/qhe,khe->hqk/dot_general | solution.py:100
  115.7 3.3 copy.74
  119.0 3.2 reshape.514
  122.2 2.7 add_dynamic-update-slice_fusion.2
  130.5 5.8 %fusion.85 = (f32[512]{0:T(512)S(1)}, f32[512,2816]{1,0:T(8,128)S(1)}) fusion(bf16[512,64]{1,0:T(8,128)(2,1)S(1)} %bitcast.150, bf16[2816,1,2,64]{3,0,2,1:T(8,128)(2,1)S(1)} %bitcast.143, pred[2816]{0:T(1024)(128)(4,1)S(1)} %gt.22, s32[2816]{0:T(1024)S(1)} %get-tuple-element.564, s32[512]{0:T(512)S(1)} %get-tuple-element.565, ...), kind=kOutput, calls=%fused_computation.123.clone.1 | convolution fusion | flops 214826496 | bytes 6667264 | tf_op jit(solution)/shard_map/while/body/eval_jaxpr/qhe,khe->hqk/dot_general | solution.py:100
  147.8 3.3 copy.74
  151.1 3.2 reshape.514
  154.3 2.7 add_dynamic-update-slice_fusion.2
  162.6 5.8 %fusion.85 = (f32[512]{0:T(512)S(1)}, f32[512,2816]{1,0:T(8,128)S(1)}) fusion(bf16[512,64]{1,0:T(8,128)(2,1)S(1)} %bitcast.150, bf16[2816,1,2,64]{3,0,2,1:T(8,128)(2,1)S(1)} %bitcast.143, pred[2816]{0:T(1024)(128)(4,1)S(1)} %gt.22, s32[2816]{0:T(1024)S(1)} %get-tuple-element.564, s32[512]{0:T(512)S(1)} %get-tuple-element.565, ...), kind=kOutput, calls=%fused_computation.123.clone.1 | convolution fusion | flops 214826496 | bytes 6667264 | tf_op jit(solution)/shard_map/while/body/eval_jaxpr/qhe,khe->hqk/dot_general | solution.py:100
  179.9 3.3 copy.74
  183.2 3.2 reshape.514
  186.3 2.7 add_dynamic-update-slice_fusion.2
  191.1 3.6 %collective-permute-start.8 = (bf16[3,22,16,128]{3,2,1,0:T(8,128)(2,1)S(1)}, bf16[3,22,16,128]{3,2,1,0:T(8,128)(2,1)S(1)}, u32[]{:S(2)}, u32[]{:S(2)}) collective-permute-start(bf16[3,22,16,128]{3,2,1,0:T(8,128)(2,1)S(1)} %get-tuple-element.399), channel_id=1, source_target_pairs={{0,16},{16,32},{32,48},{48,64},{64,80},{80,96},{96,112},{1,17},{17... | collective-permute-start | bytes 811016 | tf_op jit(solution)/shard_map/ppermute | solution.py:15
  198.6 7.3 %collective-permute-done.9 = bf16[3,22,16,128]{3,2,1,0:T(8,128)(2,1)S(1)} collective-permute-done((bf16[3,22,16,128]{3,2,1,0:T(8,128)(2,1)S(1)}, bf16[3,22,16,128]{3,2,1,0:T(8,128)(2,1)S(1)}, u32[]{:S(2)}, u32[]{:S(2)}) %collective-permute-start.9) | collective-permute-done | bytes 270368 | tf_op jit(solution)/shard_map/ppermute | solution.py:18
  207.0 6.8 %collective-permute-start.10 = (bf16[8,3,16,128]{3,2,1,0:T(8,128)(2,1)}, bf16[8,3,16,128]{3,2,1,0:T(8,128)(2,1)}, u32[]{:S(2)}, u32[]{:S(2)}) collective-permute-start(bf16[8,3,16,128]{3,2,1,0:T(8,128)(2,1)} %get-tuple-element.405), channel_id=1, source_target_pairs={{0,4},{4,8},{8,12},{1,5},{5,9},{9,13},{2,6},{6,10},{10,14},{3,7},{... | collective-permute-start | bytes 294920 | tf_op jit(solution)/shard_map/ppermute | solution.py:15
  217.0 3.1 collective-permute-done.11
  230.5 4.1 %convert_element_type.112 = bf16[8,16,16,192]{3,2,1,0:T(8,128)(2,1)S(1)} reshape(bf16[2048,1,3,64]{3,2,0,1:T(4,128)(2,1)} %copy.55) | data formatting | bytes 1572864 | tf_op jit(solution)/shard_map/convert_element_type | solution.py:172
  237.0 20.4 %copy.58 = f32[8,16,16,384]{2,1,0,3:T(8,128)} copy(f32[8,16,16,384]{3,2,1,0:T(8,128)} %fusion.14) | data formatting | bytes 6291456
  257.4 21.8 %reshape.511 = f32[384,2048]{1,0:T(8,128)} reshape(f32[384,8,16,16]{3,2,1,0:T(8,128)} %bitcast.147) | data formatting | bytes 6291456
  282.0 32.6 %psum.22 = bf16[64,384]{1,0:T(8,128)(2,1)S(1)} all-reduce(bf16[64,384]{1,0:T(8,128)(2,1)S(1)} %fusion.9), channel_id=1, replica_groups=mesh['gx'=8,'gy'=4,'ha'=4] {'gx'}, use_global_device_ids=true, to_apply=%region_7.8 | all-reduce | flops 24576 | bytes 98304 | tf_op jit(solution)/shard_map/psum | solution.py:189
  314.7 14.8 %psum.23 = bf16[64,384]{1,0:T(8,128)(2,1)S(1)} all-reduce(bf16[64,384]{1,0:T(8,128)(2,1)S(1)} %psum.22), channel_id=1, replica_groups=mesh['gx'=8,'gy'=4,'ha'=4] {'gy'}, use_global_device_ids=true, to_apply=%region_8.9 | all-reduce | flops 24576 | bytes 98304 | tf_op jit(solution)/shard_map/psum | solution.py:189
  330.1 3.4 all-reduce.2.cloned.1.call-done
  335.2 4.7 %reshape.512 = bf16[96,8,16,16]{3,2,1,0:T(8,128)(2,1)} reshape(f32[96,2048]{1,0:T(8,128)} %reduce-scatter.4.cloned.1.call-done) | data formatting | bytes 1179648
  339.8 4.8 %copy.59 = bf16[8,16,16,96]{3,2,1,0:T(8,128)(2,1)} copy(bf16[8,16,16,96]{2,1,0,3:T(8,128)(2,1)} %bitcast.154) | data formatting | bytes 786432
  (190 shorter events, 133.2 us)
Async XLA Ops:
  8.0 7.8 %copy-start = (bf16[8,16,16,384]{3,2,1,0:T(8,128)(2,1)S(1)}, bf16[8,16,16,384]{3,2,1,0:T(8,128)(2,1)}, u32[]{:S(2)}) copy-start(bf16[8,16,16,384]{3,2,1,0:T(8,128)(2,1)} %param.15) | copy-start | bytes 4718596
  8.0 325.5 %all-reduce.2.cloned.1.call-start = ((), (), s32[]{:S(2)}) async-start(), calls=%async_computation.1 | async-start | bytes 294912 | tf_op jit(solution)/shard_map/psum | solution.py:188
  10.3 5.4 %copy-start.11 = (bf16[8,16,16]{2,1,0:T(8,128)(2,1)}, bf16[8,16,16]{2,1,0:T(8,128)(2,1)S(1)}, u32[]{:S(2)}) copy-start(bf16[8,16,16]{2,1,0:T(8,128)(2,1)S(1)} %fusion.17) | copy-start | bytes 12292
  11.0 24.1 %collective-permute-start.4 = (bf16[3,16,16]{2,1,0:T(8,128)(2,1)}, bf16[3,16,16]{2,1,0:T(8,128)(2,1)S(1)}, u32[]{:S(2)}, u32[]{:S(2)}) collective-permute-start(bf16[3,16,16]{2,1,0:T(8,128)(2,1)} %get-tuple-element.409), channel_id=1, source_target_pairs={{0,16},{16,32},{32,48},{48,64},{64,80},{80,96},{96,112},{1,17},{17... | collective-permute-start | bytes 4616 | tf_op jit(solution)/shard_map/ppermute | solution.py:15
  14.5 20.6 %collective-permute-start.5 = (bf16[3,16,16]{2,1,0:T(8,128)(2,1)}, bf16[3,16,16]{2,1,0:T(8,128)(2,1)}, u32[]{:S(2)}, u32[]{:S(2)}) collective-permute-start(bf16[3,16,16]{2,1,0:T(8,128)(2,1)} %get-tuple-element.410), channel_id=1, source_target_pairs={{16,0},{32,16},{48,32},{64,48},{80,64},{96,80},{112,96},{17,1},{33... | collective-permute-start | bytes 4616 | tf_op jit(solution)/shard_map/ppermute | solution.py:18
  15.8 15.5 %copy-start.4 = (bf16[8,16,16,384]{3,2,1,0:T(8,128)(2,1)S(1)}, bf16[8,16,16,384]{3,2,1,0:T(8,128)(2,1)}, u32[]{:S(2)}) copy-start(bf16[8,16,16,384]{3,2,1,0:T(8,128)(2,1)} %param.19) | copy-start | bytes 4718596
  21.4 18.1 %collective-permute-start.1 = (bf16[3,16,16,128]{3,2,1,0:T(8,128)(2,1)}, bf16[3,16,16,128]{3,2,1,0:T(8,128)(2,1)}, u32[]{:S(2)}, u32[]{:S(2)}) collective-permute-start(bf16[3,16,16,128]{3,2,1,0:T(8,128)(2,1)} %slice.212), channel_id=1, source_target_pairs={{16,0},{32,16},{48,32},{64,48},{80,64},{96,80},{112,96},{17,1},{33... | collective-permute-start | bytes 589832 | tf_op jit(solution)/shard_map/ppermute | solution.py:18
  24.8 13.6 %collective-permute-start = (bf16[3,16,16,128]{3,2,1,0:T(8,128)(2,1)}, bf16[3,16,16,128]{3,2,1,0:T(8,128)(2,1)}, u32[]{:S(2)}, u32[]{:S(2)}) collective-permute-start(bf16[3,16,16,128]{3,2,1,0:T(8,128)(2,1)} %slice.209), channel_id=1, source_target_pairs={{0,16},{16,32},{32,48},{48,64},{64,80},{80,96},{96,112},{1,17},{17... | collective-permute-start | bytes 589832 | tf_op jit(solution)/shard_map/ppermute | solution.py:15
  32.7 2.4 copy-start.12
  35.8 16.2 %collective-permute-start.6 = (bf16[14,3,16]{2,1,0:T(4,128)(2,1)S(1)}, bf16[14,3,16]{2,1,0:T(4,128)(2,1)S(1)}, u32[]{:S(2)}, u32[]{:S(2)}) collective-permute-start(bf16[14,3,16]{2,1,0:T(4,128)(2,1)S(1)} %get-tuple-element.407), channel_id=1, source_target_pairs={{0,4},{4,8},{8,12},{1,5},{5,9},{9,13},{2,6},{6,10},{10,14},{3,7},{... | collective-permute-start | bytes 4040 | tf_op jit(solution)/shard_map/ppermute | solution.py:15
  37.1 14.9 %collective-permute-start.7 = (bf16[14,3,16]{2,1,0:T(4,128)(2,1)S(1)}, bf16[14,3,16]{2,1,0:T(4,128)(2,1)S(1)}, u32[]{:S(2)}, u32[]{:S(2)}) collective-permute-start(bf16[14,3,16]{2,1,0:T(4,128)(2,1)S(1)} %get-tuple-element.408), channel_id=1, source_target_pairs={{4,0},{8,4},{12,8},{5,1},{9,5},{13,9},{6,2},{10,6},{14,10},{7,3},{... | collective-permute-start | bytes 4040 | tf_op jit(solution)/shard_map/ppermute | solution.py:18
  41.4 12.0 %collective-permute-start.2 = (bf16[14,3,16,128]{3,2,1,0:T(8,128)(2,1)S(1)}, bf16[14,3,16,128]{3,2,1,0:T(8,128)(2,1)S(1)}, u32[]{:S(2)}, u32[]{:S(2)}) collective-permute-start(bf16[14,3,16,128]{3,2,1,0:T(8,128)(2,1)S(1)} %get-tuple-element.401), channel_id=1, source_target_pairs={{0,4},{4,8},{8,12},{1,5},{5,9},{9,13},{2,6},{6,10},{10,14},{3,7},{... | collective-permute-start | bytes 516104 | tf_op jit(solution)/shard_map/ppermute | solution.py:15
  47.6 6.2 %collective-permute-start.3 = (bf16[14,3,16,128]{3,2,1,0:T(8,128)(2,1)S(1)}, bf16[14,3,16,128]{3,2,1,0:T(8,128)(2,1)}, u32[]{:S(2)}, u32[]{:S(2)}) collective-permute-start(bf16[14,3,16,128]{3,2,1,0:T(8,128)(2,1)S(1)} %get-tuple-element.402), channel_id=1, source_target_pairs={{4,0},{8,4},{12,8},{5,1},{9,5},{13,9},{6,2},{10,6},{14,10},{7,3},{... | collective-permute-start | bytes 516104 | tf_op jit(solution)/shard_map/ppermute | solution.py:18
  57.3 3.5 copy-start.13
  74.5 1.6 copy-start.1
  77.3 2.7 copy-start.2
  106.6 1.6 copy-start.1
  109.3 2.7 copy-start.2
  138.7 1.6 copy-start.1
  141.4 2.7 copy-start.2
  170.8 1.6 copy-start.1
  173.5 2.7 copy-start.2
  189.0 7.0 %copy-start.3 = (f32[14,22,16,128]{3,2,1,0:T(8,128)S(1)}, f32[14,22,16,128]{3,2,1,0:T(8,128)}, u32[]{:S(2)}) copy-start(f32[14,22,16,128]{3,2,1,0:T(8,128)} %get-tuple-element.223) | copy-start | bytes 7569412
  191.1 7.5 %collective-permute-start.8 = (bf16[3,22,16,128]{3,2,1,0:T(8,128)(2,1)S(1)}, bf16[3,22,16,128]{3,2,1,0:T(8,128)(2,1)S(1)}, u32[]{:S(2)}, u32[]{:S(2)}) collective-permute-start(bf16[3,22,16,128]{3,2,1,0:T(8,128)(2,1)S(1)} %get-tuple-element.399), channel_id=1, source_target_pairs={{0,16},{16,32},{32,48},{48,64},{64,80},{80,96},{96,112},{1,17},{17... | collective-permute-start | bytes 811016 | tf_op jit(solution)/shard_map/ppermute | solution.py:15
  194.7 11.3 %collective-permute-start.9 = (bf16[3,22,16,128]{3,2,1,0:T(8,128)(2,1)S(1)}, bf16[3,22,16,128]{3,2,1,0:T(8,128)(2,1)S(1)}, u32[]{:S(2)}, u32[]{:S(2)}) collective-permute-start(bf16[3,22,16,128]{3,2,1,0:T(8,128)(2,1)S(1)} %get-tuple-element.400), channel_id=1, source_target_pairs={{16,0},{32,16},{48,32},{64,48},{80,64},{96,80},{112,96},{17,1},{33... | collective-permute-start | bytes 811016 | tf_op jit(solution)/shard_map/ppermute | solution.py:18
  206.0 9.0 %copy-start.8 = (bf16[8,16,16,64]{3,2,1,0:T(8,128)(2,1)S(1)}, bf16[8,16,16,64]{3,2,1,0:T(8,128)(2,1)}, u32[]{:S(2)}) copy-start(bf16[8,16,16,64]{3,2,1,0:T(8,128)(2,1)} %get-tuple-element.222) | copy-start | bytes 786436
  207.0 10.1 %collective-permute-start.10 = (bf16[8,3,16,128]{3,2,1,0:T(8,128)(2,1)}, bf16[8,3,16,128]{3,2,1,0:T(8,128)(2,1)}, u32[]{:S(2)}, u32[]{:S(2)}) collective-permute-start(bf16[8,3,16,128]{3,2,1,0:T(8,128)(2,1)} %get-tuple-element.405), channel_id=1, source_target_pairs={{0,4},{4,8},{8,12},{1,5},{5,9},{9,13},{2,6},{6,10},{10,14},{3,7},{... | collective-permute-start | bytes 294920 | tf_op jit(solution)/shard_map/ppermute | solution.py:15
  213.7 6.3 %collective-permute-start.11 = (bf16[8,3,16,128]{3,2,1,0:T(8,128)(2,1)}, bf16[8,3,16,128]{3,2,1,0:T(8,128)(2,1)}, u32[]{:S(2)}, u32[]{:S(2)}) collective-permute-start(bf16[8,3,16,128]{3,2,1,0:T(8,128)(2,1)} %get-tuple-element.406), channel_id=1, source_target_pairs={{4,0},{8,4},{12,8},{5,1},{9,5},{13,9},{6,2},{10,6},{14,10},{7,3},{... | collective-permute-start | bytes 294920 | tf_op jit(solution)/shard_map/ppermute | solution.py:18
  217.0 9.6 %copy-start.9 = (bf16[2048,1,1,64]{0,3,2,1:T(8,128)(2,1)S(1)}, bf16[2048,1,1,64]{0,3,2,1:T(8,128)(2,1)}, u32[]{:S(2)}) copy-start(bf16[2048,1,1,64]{0,3,2,1:T(8,128)(2,1)} %copy.53) | copy-start | bytes 786436
  229.2 5.4 %copy-start.10 = (bf16[384,192]{0,1:T(8,128)(2,1)S(1)}, bf16[384,192]{0,1:T(8,128)(2,1)}, u32[]{:S(2)}) copy-start(bf16[384,192]{0,1:T(8,128)(2,1)} %param.16) | copy-start | bytes 442372
  230.5 104.7 %reduce-scatter.4.cloned.1.call-start = ((), (), s32[]{:S(2)}) async-start(), calls=%async_computation.2 | async-start | bytes 3932160
  279.2 1.4 copy-start.5
  (2 other events, 1.9 us)
Sparse Core Ops, SparseCore 0:
  230.6 102.9 all-reduce.1
Sparse Core Ops, SparseCore 1:
  279.3 42.7 reduce-scatter.3
